TPU v7x, 32 devices: a whole 2x2x4 slice. The times are simulated.
32 devices in a mesh: grp: 2 (over x), seq: 8 (over z, y), ten: 2 (over core).
Axes of the slice: x: 2, y: 2, z: 4, core: 2. Of those that a mesh axis runs over, the one named last changes fastest.
Arguments:
- queries: bfloat16 [1024, 4096], P(('grp', 'seq'), 'ten'), parts along dimension 0, may hold values from -128 to 128
- keys: bfloat16 [1024, 512], P(('grp', 'seq'), 'ten'), parts along dimension 0, may hold values from -6 to 6
- values: bfloat16 [1024, 512], P(('grp', 'seq'), 'ten'), parts along dimension 0, may hold values from -6 to 6
- hidden: bfloat16 [1024, 8192], P(('grp', 'seq')), parts along dimension 0, may hold values from -6 to 6
- norm_gain: float32 [8192], replicated, may hold values from 0.1 to 1.9
- retained_lists: int32 [1024], P(('grp', 'seq')), parts along dimension 0, may hold values from -1 to 63, as said below
- counts: int32 [16], P('grp'), parts along dimension 0, may hold values from 0 to 64, as said below
- affine_matrix: bfloat16 [8192, 5120], P('seq', 'ten'), may hold values from -0.0625 to 0.0625
- affine_offset_vector: float32 [5120], P('ten'), may hold values from -3 to 3
Outputs:
- context: float32 [1024, 4096], P(('grp', 'seq'), 'ten'), parts along dimension 0
- col_scores: float32 [1024], P(('grp', 'seq')), parts along dimension 0
- tier_third_mapped_triples: float32 [512, 5120], P(('grp', 'seq'), 'ten'), parts along dimension 0
There are 2 independent parts, one for each index of `grp`. A program takes and returns all parts, laid end to end along the dimension named above; an argument that names none is the same for every part. Nothing has to cross between parts.
Inputs may be any that keep to these rules, and one draw needn't show every extreme that they name: `retained_lists`: entries s*64 to (s+1)*64 - 1 hold, in their first counts[s] places, the kept local rows of shard s in rising order, and -1 after them. counts sum to 256; some shard keeps all its 64 rows.
All inputs are finite; a program needn't handle non-finite values.
Results may differ from a plain program's by a relative error of at most 0.0027.
Values may be sent and summed in bfloat16 or wider, within the bound.
A program may use at most 64 MiB of HBM per device.

v0:
```python
import math

import jax
import jax.numpy as jnp
from jax import lax
from jax.sharding import PartitionSpec as P

HEAD_SIZE = 128
QUERY_HEADS = 32


def block_length(key_count):
    return math.gcd(key_count, 512)


def heads_first(queries, kv_heads):
    partition_inner_lines = queries.shape[0]
    group_width = queries.shape[1] // (HEAD_SIZE * kv_heads)
    return (
        queries.reshape(partition_inner_lines, kv_heads, group_width, HEAD_SIZE)
        .transpose(1, 2, 0, 3)
        .reshape(kv_heads, group_width * partition_inner_lines, HEAD_SIZE)
    )


def masked_scores(query_heads, query_pos, key_block, offset):
    key_count = key_block.shape[0]
    kv_heads = query_heads.shape[0]
    key_head_rows = key_block.reshape(key_count, kv_heads, HEAD_SIZE)
    scores = jnp.einsum(
        "hrd,nhd->hrn", query_heads, key_head_rows, preferred_element_type=jnp.float32
    ) * HEAD_SIZE ** (-0.5)
    key_pos = offset + jnp.arange(key_count, dtype=jnp.int32)
    allowed = key_pos[None, None, :] <= query_pos[None, :, None]
    return (scores, allowed)


def attend(carried, pieces, query_heads, query_pos):
    key_piece, value_piece = pieces
    key_count = key_piece.shape[0]
    block_rows = block_length(key_count)
    block_total = key_count // block_rows
    kv_heads = query_heads.shape[0]
    key_blocks = key_piece.reshape(block_total, block_rows, key_piece.shape[1])
    value_blocks = value_piece.reshape(block_total, block_rows, value_piece.shape[1])

    def attend_step_block(state, inputs):
        row_max, row_sum, accumulated = state
        key_block, value_block, token_count = inputs
        scores, allowed = masked_scores(query_heads, query_pos, key_block, token_count * block_rows)
        new_max = jnp.maximum(row_max, jnp.max(jnp.where(allowed, scores, -1e30), axis=2))
        weights = jnp.where(allowed, jnp.exp(scores - new_max[:, :, None]), 0.0)
        factor = jnp.exp(row_max - new_max)
        row_sum = row_sum * factor + jnp.sum(weights, axis=2)
        value_head_rows = value_block.reshape(block_rows, kv_heads, HEAD_SIZE)
        update = jnp.einsum(
            "hrn,nhd->hrd",
            weights.astype(jnp.bfloat16),
            value_head_rows,
            preferred_element_type=jnp.float32,
        )
        accumulated = accumulated * factor[:, :, None] + update
        return ((new_max, row_sum, accumulated), None)

    state, unused = lax.scan(
        attend_step_block,
        carried,
        (key_blocks, value_blocks, jnp.arange(block_total, dtype=jnp.int32)),
    )
    return state


def column_terms(key_piece, query_heads, query_pos, log_total):
    key_count = key_piece.shape[0]
    block_rows = block_length(key_count)
    block_total = key_count // block_rows
    key_blocks = key_piece.reshape(block_total, block_rows, key_piece.shape[1])

    def column_step_block(state, inputs):
        key_block, token_count = inputs
        scores, allowed = masked_scores(query_heads, query_pos, key_block, token_count * block_rows)
        weights = jnp.where(allowed, jnp.exp(scores - log_total[:, :, None]), 0.0)
        return (state, jnp.sum(weights, axis=(0, 1)))

    unused, sums = lax.scan(
        column_step_block, jnp.float32(0.0), (key_blocks, jnp.arange(block_total, dtype=jnp.int32))
    )
    return sums.reshape(key_count)


def shards(
    queries,
    keys,
    values,
    hidden,
    norm_gain,
    retained_lists,
    counts,
    affine_matrix,
    affine_offset_vector,
):
    partition_inner_lines = queries.shape[0]
    kv_heads = keys.shape[1] // HEAD_SIZE
    group_width = queries.shape[1] // keys.shape[1]
    seq_index = lax.axis_index("seq")
    query_heads = heads_first(queries, kv_heads)
    query_pos = seq_index * partition_inner_lines + jnp.tile(
        jnp.arange(partition_inner_lines, dtype=jnp.int32), group_width
    )
    packed_rows = group_width * partition_inner_lines
    initial = (
        jnp.full((kv_heads, packed_rows), -1e30, jnp.float32),
        jnp.zeros((kv_heads, packed_rows), jnp.float32),
        jnp.zeros((kv_heads, packed_rows, HEAD_SIZE), jnp.float32),
    )
    row_max, row_sum, accumulated = attend(
        initial,
        (
            lax.all_gather(keys, "seq", axis=0, tiled=True),
            lax.all_gather(values, "seq", axis=0, tiled=True),
        ),
        query_heads,
        query_pos,
    )
    log_total = row_max + jnp.log(row_sum)
    column_part = column_terms(
        lax.all_gather(keys, "seq", axis=0, tiled=True), query_heads, query_pos, log_total
    )
    context = (
        (accumulated / row_sum[:, :, None])
        .reshape(kv_heads, group_width, partition_inner_lines, HEAD_SIZE)
        .transpose(2, 0, 1, 3)
        .reshape(partition_inner_lines, queries.shape[1])
    )
    column_rows = lax.psum_scatter(column_part, "seq", scatter_dimension=0, tiled=True)
    col_scores = lax.psum(column_rows, "ten") / QUERY_HEADS
    hidden_f = hidden.astype(jnp.float32)
    rescaled_activations = (
        hidden_f
        * lax.rsqrt(jnp.mean(hidden_f * hidden_f, axis=1, keepdims=True) + 1e-06)
        * norm_gain
    ).astype(jnp.bfloat16)
    selector = (
        retained_lists[:, None] == jnp.arange(partition_inner_lines, dtype=jnp.int32)[None, :]
    ).astype(jnp.bfloat16)
    chosen = jnp.dot(selector, rescaled_activations, preferred_element_type=jnp.float32).astype(
        jnp.bfloat16
    )
    sequence_total = lax.axis_size("seq")
    retained_total = sequence_total * partition_inner_lines // 2
    retained_element = jnp.arange(retained_total, dtype=jnp.int32)
    partition_finish_marks = jnp.cumsum(counts)
    holder_partition = jnp.sum(
        (partition_finish_marks[None, :] <= retained_element[:, None]).astype(jnp.int32), axis=1
    )
    starts = partition_finish_marks - counts
    opening_marks = jnp.sum(
        jnp.where(
            jnp.arange(sequence_total, dtype=jnp.int32)[None, :] == holder_partition[:, None],
            starts[None, :],
            0,
        ),
        axis=1,
    )
    retained_place_number = retained_element - opening_marks
    received = lax.all_to_all(chosen, "seq", split_axis=1, concat_axis=0, tiled=True)
    provenance = holder_partition * partition_inner_lines + retained_place_number
    compact = jnp.take(received, provenance, axis=0)
    projected = lax.psum_scatter(
        jnp.dot(compact, affine_matrix, preferred_element_type=jnp.float32),
        "seq",
        scatter_dimension=0,
        tiled=True,
    )
    tier_third_mapped_triples = projected + affine_offset_vector
    return (context, col_scores, tier_third_mapped_triples)


def solution(mesh):
    in_specs = (
        P(("grp", "seq"), "ten"),
        P(("grp", "seq"), "ten"),
        P(("grp", "seq"), "ten"),
        P(("grp", "seq"), None),
        P(),
        P(("grp", "seq")),
        P("grp"),
        P("seq", "ten"),
        P("ten"),
    )
    out_specs = (P(("grp", "seq"), "ten"), P(("grp", "seq")), P(("grp", "seq"), "ten"))
    return jax.shard_map(shards, mesh=mesh, in_specs=in_specs, out_specs=out_specs, check_vma=False)
```

profile of v0, /device:TPU:0, one launch (start us, length us, event | category | flops | bytes accessed | tf_op | source)
XLA Modules:
  0.0 152.0 jit_solution(15588536419003187684)
XLA Ops:
  7.2 1.5 %fusion = f32[64]{0:T(128)S(1)} fusion(bf16[64,8192]{1,0:T(8,128)(2,1)} %param.12), kind=kLoop, calls=%fused_computation.4 | loop fusion | flops 1572800 | bytes 1048832 | tf_op jit(solution)/shard_map/reduce_sum | solution.py:140
  8.7 1.7 %convolution_convert_fusion = bf16[64,8192]{1,0:T(8,128)(2,1)S(1)} fusion(bf16[64,8192]{1,0:T(8,128)(2,1)} %param.12, f32[8192]{0:T(1024)} %param.13, f32[64]{0:T(128)S(1)} %add_rsqrt_fusion, s32[64]{0:T(128)} %param.14), kind=kOutput, calls=%fused_computation.1 | convolution fusion | flops 69734400 | bytes 2130432 | tf_op jit(solution)/shard_map/dot_general | solution.py:146
  10.5 0.0 copy-start.4
  10.5 1.1 copy.48
  11.6 7.3 %all-to-all-start = ((bf16[64,8,1024]{2,0,1:T(8,128)(2,1)}), bf16[64,8,1024]{2,0,1:T(8,128)(2,1)S(1)}, u32[]{:S(2)}, u32[]{:S(2)}) async-start(bf16[64,8,1024]{2,0,1:T(8,128)(2,1)} %bitcast.32), calls=%async_computation | async-start | bytes 2097152 | tf_op jit(solution)/shard_map/all_to_all | solution.py:166
  18.9 0.0 reduce-scatter.2.cloned.1.call-start
  18.9 0.0 copy-done.4
  18.9 0.2 reduce-window.8
  19.1 0.1 convert_reduce_fusion
  19.2 0.1 select_reduce_fusion.2
  19.3 25.3 %all-to-all-done = bf16[64,8,1024]{2,0,1:T(8,128)(2,1)S(1)} async-done(((bf16[64,8,1024]{2,0,1:T(8,128)(2,1)}), bf16[64,8,1024]{2,0,1:T(8,128)(2,1)S(1)}, u32[]{:S(2)}, u32[]{:S(2)}) %all-to-all-start) | async-done | bytes 1048608 | tf_op jit(solution)/shard_map/all_to_all | solution.py:166
  44.6 1.2 gather_fusion
  45.8 5.6 %fusion.14 = f32[256,2560]{1,0:T(8,128)} fusion(bf16[1024,2560]{1,0:T(8,128)(2,1)} %param.16, bf16[256,1024]{1,0:T(8,128)(2,1)S(1)} %gather_fusion, pred[256]{0:T(512)(128)(4,1)S(1)} %compare_and_fusion), kind=kOutput, calls=%fused_computation.23 | convolution fusion | flops 1342439424 | bytes 8388864 | tf_op jit(solution)/shard_map/dot_general | solution.py:170
  51.4 0.0 copy-start
  51.4 0.0 copy-start.1
  51.4 0.0 copy-start.2
  51.4 0.0 reduce-scatter.2.cloned.1.call-update
  51.4 0.1 add.110
  51.5 0.8 copy-done
  52.4 0.1 copy.32
  52.4 0.0 copy-done.1
  52.4 31.7 %all_gather.7 = bf16[512,256]{1,0:T(8,128)(2,1)S(1)} all-gather(bf16[64,256]{1,0:T(8,128)(2,1)S(1)} %copy-done.1), channel_id=1, replica_groups=mesh['grp'=2,'seq'=8,'ten'=2] {'seq'}, dimensions={0}, use_global_device_ids=true | all-gather | bytes 294912 | tf_op jit(solution)/shard_map/all_gather | solution.py:119
  84.2 0.1 copy.33
  84.3 0.0 copy-done.2
  84.3 31.4 %all_gather.8 = bf16[512,256]{1,0:T(8,128)(2,1)S(1)} all-gather(bf16[64,256]{1,0:T(8,128)(2,1)S(1)} %copy-done.2), channel_id=1, replica_groups=mesh['grp'=2,'seq'=8,'ten'=2] {'seq'}, dimensions={0}, use_global_device_ids=true | all-gather | bytes 294912 | tf_op jit(solution)/shard_map/all_gather | solution.py:120
  115.7 0.1 copy.35
  115.9 0.2 iota_compare_fusion
  116.0 0.6 select_reduce_fusion.1
  116.7 0.5 fusion.3
  117.2 0.9 fusion.5
  118.2 0.0 copy-start.5
  118.2 0.0 copy-start.3
  118.2 0.3 copy.38
  118.5 1.0 copy.49
  119.5 0.0 copy-done.5
  119.5 0.6 dynamic-slice.2
  120.7 0.6 select_reduce_fusion
  121.3 19.1 %all-reduce = f32[512]{0:T(512)S(1)} all-reduce(f32[512]{0:T(512)S(1)} %select_reduce_fusion), channel_id=2, replica_groups=mesh['grp'=2,'seq'=8,'ten'=2] {'seq'}, use_global_device_ids=true, to_apply=%region_3.4.clone | all-reduce | flops 512 | bytes 4096
  140.4 0.1 dynamic-slice.3
  140.4 2.4 %psum.7 = f32[64]{0:T(128)S(1)} all-reduce(f32[64]{0:T(128)S(1)} %dynamic-slice.3), channel_id=1, replica_groups=mesh['grp'=2,'seq'=8,'ten'=2] {'ten'}, use_global_device_ids=true, to_apply=%region_4.5 | all-reduce | flops 64 | bytes 512 | tf_op jit(solution)/shard_map/psum | solution.py:136
  142.9 0.5 broadcast_multiply_fusion.1
  143.4 0.0 reduce-scatter.2.cloned.1.call-done
  143.4 0.0 copy-done.3
  143.4 1.7 %broadcast_add_fusion = f32[32,2560]{1,0:T(8,128)} fusion(f32[32,2560]{1,0:T(8,128)} %reduce-scatter.2.cloned.1.call-done, f32[2560]{0:T(1024)S(1)} %copy-done.3), kind=kLoop, calls=%fused_computation.27 | loop fusion | flops 81920 | bytes 665600 | tf_op jit(solution)/shard_map/add | solution.py:175
  (10 shorter events, 0.1 us)
Async XLA Ops:
  10.5 8.5 %copy-start.4 = (s32[8]{0:T(128)S(1)}, s32[8]{0:T(128)}, u32[]{:S(2)}) copy-start(s32[8]{0:T(128)} %param.15) | copy-start | bytes 100
  11.6 33.1 %all-to-all-start = ((bf16[64,8,1024]{2,0,1:T(8,128)(2,1)}), bf16[64,8,1024]{2,0,1:T(8,128)(2,1)S(1)}, u32[]{:S(2)}, u32[]{:S(2)}) async-start(bf16[64,8,1024]{2,0,1:T(8,128)(2,1)} %bitcast.32), calls=%async_computation | async-start | bytes 2097152 | tf_op jit(solution)/shard_map/all_to_all | solution.py:166
  18.9 124.5 %reduce-scatter.2.cloned.1.call-start = ((), (), s32[]{:S(2)}) async-start(), calls=%async_computation.2 | async-start | bytes 2949120 | tf_op jit(solution)/shard_map/reduce_scatter | solution.py:169
  51.4 0.9 copy-start
  51.4 1.1 copy-start.1
  51.4 32.9 %copy-start.2 = (bf16[64,256]{1,0:T(8,128)(2,1)S(1)}, bf16[64,256]{1,0:T(8,128)(2,1)}, u32[]{:S(2)}) copy-start(bf16[64,256]{1,0:T(8,128)(2,1)} %param.11) | copy-start | bytes 98308
  118.2 1.3 copy-start.5
  118.2 25.2 %copy-start.3 = (f32[2560]{0:T(1024)S(1)}, f32[2560]{0:T(1024)}, u32[]{:S(2)}) copy-start(f32[2560]{0:T(1024)} %param.17) | copy-start | bytes 30724
Sparse Core Ops, SparseCore 0:
  51.5 72.2 reduce-scatter.1
where the time goes:
time: 152 us
  blocking collectives  84.7 us (56%)
  waiting for transfers between devices  25.3 us (17%)
  between operations  14.8 us (10%)
  matrix products  8.9 us (6%)
  starting transfers between devices  7.35 us (5%)
  local copies, waits for them, and re-layouts  5.49 us (4%)
  other arithmetic  5.4 us (4%)
    all_gather x1, blocking collectives, shards(): lax.all_gather(keys, 'seq', axis=0, tiled=True)  31.7 us
    all_gather x1, blocking collectives, shards(): lax.all_gather(values, 'seq', axis=0, tiled=True)  31.4 us
    all_to_all x1, waiting for transfers between devices, shards(): lax.all_to_all(chosen, 'seq', split_axis=1, concat_axis=0, tiled=True)  25.3 us
    unnamed x1, blocking collectives  19.1 us
    all_to_all x1, starting transfers between devices, shards(): lax.all_to_all(chosen, 'seq', split_axis=1, concat_axis=0, tiled=True)  7.31 us
    dot_general x1, matrix products, shards(): jnp.dot(compact, affine_matrix, preferred_element_type=jnp.float32)  5.57 us
  transfers between devices with their start and end apart: 2, of which 1 were waited for; matrix products, arithmetic and copies ran while one was open for 4% of the time, Pallas kernels for 0%

commit v1 on v0

v1 whole, which is shorter than its diff:
```python
import functools
import math

import jax
import jax.numpy as jnp
from jax import lax
from jax.experimental import pallas as pl
from jax.experimental.pallas import tpu as pltpu
from jax.sharding import PartitionSpec as P

HEAD_SIZE = 128
QUERY_HEADS = 32
F32 = jnp.float32
BF16 = jnp.bfloat16


def remote(src, dst, send_sem, recv_sem, where):
    return pltpu.make_async_remote_copy(
        src_ref=src,
        dst_ref=dst,
        send_sem=send_sem,
        recv_sem=recv_sem,
        device_id=where,
        device_id_type=pl.DeviceIdType.MESH,
    )


def kernel(
    n,
    q_ref, k_ref, v_ref, h_ref, gain_ref, list_ref, count_ref, a_hbm, bias_ref,
    ctx_ref, col_ref, out_ref,
    a_ref, kbuf, vbuf, s_ref, e_ref, sel_send, sel_recv, g_ref, comp_ref,
    y_send, y_recv, own_ref, z_send, z_recv, c_send, c_recv, ct_send, ct_recv,
    a_sem, kv_ssem, kv_rsem, sv_ssem, sv_rsem, fw_ssem, fw_rsem,
    y_ssem, y_rsem, z_ssem, z_rsem, c_ssem, c_rsem, ct_ssem, ct_rsem,
):
    me = lax.axis_index("seq")
    ten = lax.axis_index("ten")
    sibling = {"ten": 1 - ten}
    rows = q_ref.shape[0]
    key_total = n * rows
    kv_heads = k_ref.shape[1] // HEAD_SIZE
    group = q_ref.shape[1] // k_ref.shape[1]
    width = h_ref.shape[1]
    half = width // n // 2
    out_rows = out_ref.shape[0]
    chunk = y_recv.shape[2]
    chunks = y_recv.shape[0]
    pairs = n // 2
    parity = lax.rem(me, 2)
    pair = lax.div(me, 2)
    partner = {"seq": me + 1 - 2 * parity}

    a_copy = pltpu.make_async_copy(a_hbm, a_ref, a_sem)
    a_copy.start()
    kbuf[...] = jnp.zeros_like(kbuf)
    vbuf[...] = jnp.zeros_like(vbuf)
    kbuf[me] = k_ref[...]
    vbuf[me] = v_ref[...]

    barrier = pltpu.get_barrier_semaphore()
    for d in range(1, n):
        pl.semaphore_signal(
            barrier, inc=1, device_id={"seq": lax.rem(me + d, n)},
            device_id_type=pl.DeviceIdType.MESH,
        )
    pl.semaphore_signal(
        barrier, inc=1, device_id=sibling, device_id_type=pl.DeviceIdType.MESH
    )
    pl.semaphore_wait(barrier, n)

    def kv_copies(d, source, target):
        return (
            remote(k_ref, kbuf.at[source], kv_ssem.at[0, d], kv_rsem.at[0, d], {"seq": target}),
            remote(v_ref, vbuf.at[source], kv_ssem.at[1, d], kv_rsem.at[1, d], {"seq": target}),
        )

    for d in range(1, n):

        @pl.when(me + d < n)
        def _():
            for copy in kv_copies(d, me, me + d):
                copy.start()

    square = jnp.zeros((rows, 1), F32)
    step = math.gcd(width, 1024)
    for c in range(width // step):
        x = h_ref[:, c * step:(c + 1) * step].astype(F32)
        square = square + jnp.sum(x * x, axis=1, keepdims=True)
    rescale = lax.rsqrt(square / width + 1e-06)
    lane = lax.broadcasted_iota(jnp.int32, (rows, rows), 1)
    line = lax.broadcasted_iota(jnp.int32, (rows, rows), 0)
    kept = jnp.sum(jnp.where(lane == line, list_ref[...], 0), axis=1, keepdims=True)
    selector = (kept == lane).astype(F32).astype(BF16)

    def chosen(owner):
        columns = pl.ds(pl.multiple_of(owner * (2 * half) + ten * half, 128), half)
        x = h_ref[:, columns].astype(F32) * rescale * gain_ref[:, columns]
        return jnp.dot(selector, x.astype(BF16), preferred_element_type=F32).astype(BF16)

    def sel_copy(d, source, target):
        return remote(
            sel_send.at[d], sel_recv.at[ten, source], sv_ssem.at[d], sv_rsem.at[d], {"seq": target}
        )

    for d in range(1, n):
        owner = lax.rem(me + d, n)
        sel_send[d] = chosen(owner)
        sel_copy(d, me, owner).start()
    sel_recv[ten, me] = chosen(me)

    def forward(d):
        source = lax.rem(me - d + n, n)
        block = sel_recv.at[ten, source]
        return remote(block, block, fw_ssem.at[d], fw_rsem.at[d], sibling)

    forward(0).start()

    at = lax.broadcasted_iota(jnp.int32, (1, key_total), 1)
    place = jnp.full((1, key_total), -1, jnp.int32)
    start = jnp.int32(0)
    for s in range(n):
        t = at - s * rows
        place = jnp.where((t >= 0) & (t < count_ref[s]), start + t, place)
        start = start + count_ref[s]
    row_at = lax.broadcasted_iota(jnp.int32, (out_rows, key_total), 0)
    for side in range(2):
        side_parity = 1 - parity if side == 0 else parity
        for d in range(pairs):
            base = (2 * lax.rem(pair + d, pairs) + side_parity) * out_rows
            first = (side * pairs + d) * out_rows
            g_ref[first:first + out_rows, :] = (
                (row_at + base == place).astype(F32).astype(BF16)
            )

    for d in range(1, n):

        @pl.when(me - d >= 0)
        def _():
            for copy in kv_copies(d, me - d, me):
                copy.wait_recv()

    key_pos = lax.broadcasted_iota(jnp.int32, (rows, key_total), 1)
    query_pos = me * rows + lax.broadcasted_iota(jnp.int32, (rows, key_total), 0)
    allowed = key_pos <= query_pos
    columns_total = jnp.zeros((8, key_total), F32)
    for h in range(kv_heads):
        heads = slice(h * HEAD_SIZE, (h + 1) * HEAD_SIZE)
        query = jnp.concatenate(
            [
                q_ref[:, (h * group + a) * HEAD_SIZE:(h * group + a + 1) * HEAD_SIZE]
                for a in range(group)
            ],
            axis=0,
        )
        key = kbuf[:, :, heads].reshape(key_total, HEAD_SIZE)
        value = vbuf[:, :, heads].reshape(key_total, HEAD_SIZE)
        s_ref[...] = lax.dot_general(
            query, key, (((1,), (1,)), ((), ())), preferred_element_type=F32
        )
        inverses = []
        for a in range(group):
            lines = slice(a * rows, (a + 1) * rows)
            scores = jnp.where(allowed, s_ref[lines, :] * HEAD_SIZE ** (-0.5), -1e30)
            largest = jnp.max(scores, axis=1, keepdims=True)
            weights = jnp.where(allowed, jnp.exp(scores - largest), 0.0)
            e_ref[lines, :] = weights.astype(BF16)
            inverse = 1.0 / jnp.sum(weights, axis=1, keepdims=True)
            inverses.append(inverse)
            columns_total = columns_total + jnp.sum(
                (weights * inverse).reshape(rows // 8, 8, key_total), axis=0
            )
        mixed = jnp.dot(e_ref[...], value, preferred_element_type=F32)
        for a in range(group):
            place_at = (h * group + a) * HEAD_SIZE
            ctx_ref[:, place_at:place_at + HEAD_SIZE] = (
                mixed[a * rows:(a + 1) * rows] * inverses[a]
            )
    lanes = c_send.shape[2]
    per = lanes // rows
    for b in range(n // per):
        c_send[b] = columns_total[:, b * lanes:(b + 1) * lanes]

    def col_copy(d, owner, target):
        return remote(
            c_send.at[lax.div(owner, per)], c_recv.at[d], c_ssem.at[d], c_rsem.at[d],
            {"seq": target},
        )

    for d in range(1, n):

        @pl.when(me - d >= 0)
        def _():
            col_copy(d, me - d, me - d).start()

    for d in range(1, n):
        sel_copy(d, lax.rem(me - d + n, n), me).wait_recv()
        forward(d).start()
    for d in range(n):
        source = lax.rem(me - d + n, n)
        block = sel_recv.at[1 - ten, source]
        remote(block, block, fw_ssem.at[d], fw_rsem.at[d], sibling).wait_recv()
    for side in range(2):
        comp_ref[:, side * half:(side + 1) * half] = jnp.dot(
            g_ref[...], sel_recv[side].reshape(key_total, half), preferred_element_type=F32
        ).astype(BF16)
    a_copy.wait()

    side_rows = pairs * out_rows

    def y_copy(c):
        return remote(y_send.at[c], y_recv.at[c], y_ssem.at[c], y_rsem.at[c], partner)

    def z_copy(c, d):
        target = {"seq": 2 * lax.rem(pair + d, pairs) + parity}
        return remote(
            z_send.at[c, d], z_recv.at[c, d], z_ssem.at[c, d], z_rsem.at[c, d], target
        )

    def pass_on(c):
        y_copy(c).wait_recv()
        for d in range(1, pairs):
            part = slice(d * out_rows, (d + 1) * out_rows)
            z_send[c, d] = (own_ref[c, part, :] + y_recv[c, part, :].astype(F32)).astype(BF16)
            z_copy(c, d).start()

    for c in range(chunks):
        columns = slice(c * chunk, (c + 1) * chunk)
        y_send[c] = jnp.dot(
            comp_ref[:side_rows, :], a_ref[:, columns], preferred_element_type=F32
        ).astype(BF16)
        y_copy(c).start()
        own_ref[c] = jnp.dot(
            comp_ref[side_rows:, :], a_ref[:, columns], preferred_element_type=F32
        )
        if c > 0:
            pass_on(c - 1)
    pass_on(chunks - 1)

    zero = jnp.int32(0)
    mine = c_send[lax.div(me, per)]
    for d in range(1, n):
        c_recv_valid = me + d < n

        @pl.when(c_recv_valid)
        def _():
            col_copy(d, me, me).wait_recv()

        @pl.when(jnp.logical_not(c_recv_valid))
        def _():
            c_recv[d] = jnp.zeros_like(c_recv[d])

        mine = mine + c_recv[d]
    ct_send[...] = mine
    ct = remote(ct_send, ct_recv, ct_ssem, ct_rsem, sibling)
    ct.start()

    for c in range(chunks):
        columns = slice(c * chunk, (c + 1) * chunk)
        total = own_ref[c, :out_rows, :] + y_recv[c, :out_rows, :].astype(F32)
        for d in range(1, pairs):
            z_copy(c, d).wait_recv()
            total = total + z_recv[c, d].astype(F32)
        out_ref[:, columns] = total + bias_ref[:, columns]

    ct.wait()
    both = jnp.sum(ct_send[...] + ct_recv[...], axis=0, keepdims=True) / QUERY_HEADS
    turn = lax.rem(me, per)
    picked = both[:, :rows]
    for b in range(1, per):
        picked = jnp.where(turn == b, both[:, b * rows:(b + 1) * rows], picked)
    col_ref[...] = picked

    for d in range(1, n):

        @pl.when(me + d < n)
        def _():
            for copy in kv_copies(d, me, me + d):
                copy.wait_send()

        @pl.when(me - d >= 0)
        def _():
            col_copy(d, me - d, me - d).wait_send()

        sel_copy(d, me, lax.rem(me + d, n)).wait_send()
    for d in range(n):
        forward(d).wait_send()
    for c in range(chunks):
        y_copy(c).wait_send()
        for d in range(1, pairs):
            z_copy(c, d).wait_send()


def shards(
    n, queries, keys, values, hidden, norm_gain, retained_lists, counts, affine_matrix,
    affine_offset_vector,
):
    rows, query_width = queries.shape
    width = hidden.shape[1]
    depth, columns = affine_matrix.shape
    kv_width = keys.shape[1]
    group = query_width // kv_width
    half = width // n // 2
    out_rows = rows // 2
    kept_total = n * out_rows
    chunk = math.gcd(columns, 512)
    chunks = columns // chunk
    pairs = n // 2
    lanes = max(128, rows)
    key_total = n * rows
    vmem = pl.BlockSpec(memory_space=pltpu.VMEM)
    dma = pltpu.SemaphoreType.DMA
    context, col_scores, projected = pl.pallas_call(
        functools.partial(kernel, n),
        out_shape=(
            jax.ShapeDtypeStruct((rows, query_width), F32),
            jax.ShapeDtypeStruct((1, rows), F32),
            jax.ShapeDtypeStruct((out_rows, columns), F32),
        ),
        in_specs=[
            vmem, vmem, vmem, vmem, vmem, vmem,
            pl.BlockSpec(memory_space=pltpu.SMEM),
            pl.BlockSpec(memory_space=pl.ANY),
            vmem,
        ],
        out_specs=(vmem, vmem, vmem),
        scratch_shapes=[
            pltpu.VMEM((depth, columns), BF16),
            pltpu.VMEM((n, rows, kv_width), BF16),
            pltpu.VMEM((n, rows, kv_width), BF16),
            pltpu.VMEM((group * rows, key_total), F32),
            pltpu.VMEM((group * rows, key_total), BF16),
            pltpu.VMEM((n, rows, half), BF16),
            pltpu.VMEM((2, n, rows, half), BF16),
            pltpu.VMEM((kept_total, key_total), BF16),
            pltpu.VMEM((kept_total, 2 * half), BF16),
            pltpu.VMEM((chunks, kept_total // 2, chunk), BF16),
            pltpu.VMEM((chunks, kept_total // 2, chunk), BF16),
            pltpu.VMEM((chunks, kept_total // 2, chunk), F32),
            pltpu.VMEM((chunks, pairs, out_rows, chunk), BF16),
            pltpu.VMEM((chunks, pairs, out_rows, chunk), BF16),
            pltpu.VMEM((key_total // lanes, 8, lanes), F32),
            pltpu.VMEM((n, 8, lanes), F32),
            pltpu.VMEM((8, lanes), F32),
            pltpu.VMEM((8, lanes), F32),
            dma,
            dma((2, n)), dma((2, n)),
            dma((n,)), dma((n,)),
            dma((n,)), dma((n,)),
            dma((chunks,)), dma((chunks,)),
            dma((chunks, pairs)), dma((chunks, pairs)),
            dma((n,)), dma((n,)),
            dma, dma,
        ],
        compiler_params=pltpu.CompilerParams(collective_id=0, has_side_effects=True),
    )(
        queries, keys, values, hidden, norm_gain.reshape(1, width),
        retained_lists.reshape(1, rows), counts, affine_matrix,
        affine_offset_vector.reshape(1, columns),
    )
    return (context, col_scores.reshape(rows), projected)


def solution(mesh):
    in_specs = (
        P(("grp", "seq"), "ten"),
        P(("grp", "seq"), "ten"),
        P(("grp", "seq"), "ten"),
        P(("grp", "seq"), None),
        P(),
        P(("grp", "seq")),
        P("grp"),
        P("seq", "ten"),
        P("ten"),
    )
    out_specs = (P(("grp", "seq"), "ten"), P(("grp", "seq")), P(("grp", "seq"), "ten"))
    return jax.shard_map(
        functools.partial(shards, mesh.shape["seq"]),
        mesh=mesh, in_specs=in_specs, out_specs=out_specs, check_vma=False,
    )
```

time: 152 us -> 67.8 us (0.45)
  blocking collectives: 84.7 us -> 0 us
  Pallas kernels: 0 us -> 60.8 us
  waiting for transfers between devices: 25.3 us -> 0 us
  between operations: 14.8 us -> 0.64 us
  matrix products: 8.9 us -> 0 us
  starting transfers between devices: 7.35 us -> 0 us
  other arithmetic: 5.4 us -> 0 us
    all_gather x2 -> x0, blocking collectives: 63.1 us -> none  [the longest x1 31.7 us: shards(): lax.all_gather(keys, 'seq', axis=0, tiled=True)]
    pallas_call x0 -> x1, Pallas kernels: none -> 60.8 us  [shards(): pl.pallas_call(functools.partial(kernel, n), out_shape=(jax.ShapeDtypeStr...]
    all_to_all x1 -> x0, waiting for transfers between devices: 25.3 us -> none  [shards(): lax.all_to_all(chosen, 'seq', split_axis=1, concat_axis=0, tiled=True)]
    unnamed x1 -> x0, blocking collectives: 19.1 us -> none
    dot_general x4 -> x0, matrix products: 8.9 us -> none  [the longest x1 5.57 us: shards(): jnp.dot(compact, affine_matrix, preferred_element_type=jnp.float32)]
    all_to_all x1 -> x0, starting transfers between devices: 7.31 us -> none  [shards(): lax.all_to_all(chosen, 'seq', split_axis=1, concat_axis=0, tiled=True)]
    reduce_sum x5 -> x0, other arithmetic: 2.76 us -> none  [the longest x1 1.53 us: shards(): jnp.mean(hidden_f * hidden_f, axis=1, keepdims=True) + 1e-06]
    psum x1 -> x0, blocking collectives: 2.45 us -> none  [shards(): col_scores = lax.psum(column_rows, 'ten') / QUERY_HEADS]
  transfers between devices with their start and end apart: 2 -> 0, of which waited for: 1 -> 0; matrix products, arithmetic and copies ran while one was open for 4% -> 0% of each run, Pallas kernels for 0% -> 0%
where the time goes in v1:
time: 67.8 us; the launch traced here: 67.5 us
  Pallas kernels  60.8 us (90%)
  local copies, waits for them, and re-layouts  6.07 us (9%)
    pallas_call x1, Pallas kernels, shards(): pl.pallas_call(functools.partial(kernel, n), out_shape=(jax.ShapeDtypeStr...  60.8 us
    unnamed x3, local copies, waits for them, and re-layouts  4.76 us

profile of v1, /device:TPU:0, one launch (start us, length us, event | category | flops | bytes accessed | tf_op | source)
XLA Modules:
  0.0 67.5 jit_solution(18192846979952715019)
XLA Ops:
  0.6 1.3 %reshape.20.bias_ref = f32[1,2560]{1,0:T(1,128)} reshape(f32[2560]{0:T(1024)} %param.17) | data formatting | bytes 20480 | tf_op jit(solution)/shard_map/reshape | solution.py:359
  1.9 60.8 %shard_map.112 = (f32[64,2048]{1,0:T(8,128)}, f32[1,64]{1,0:T(1,128)}, f32[32,2560]{1,0:T(8,128)}) custom-call(bf16[64,2048]{1,0:T(8,128)(2,1)} %q_ref.1, bf16[64,256]{1,0:T(8,128)(2,1)} %k_ref.1, bf16[64,256]{1,0:T(8,128)(2,1)} %v_ref.1, bf16[64,8192]{1,0:T(8,128)(2,1)} %h_ref.1, f32[1,8192]{1,0:T(1,128)} %bitcast.3, s32[1,64]{1,0:T(1,128)} %bitcast.4, ...), custom_call_target="tpu_custom_call" | custom-call | tf_op jit(solution)/shard_map/pallas_call | solution.py:313
  62.8 1.9 %copy.15 = f32[64,2048]{1,0:T(8,128)} copy(f32[64,2048]{1,0:T(8,128)} %get-tuple-element.12) | data formatting | bytes 1048576
  64.6 1.2 %copy.16 = f32[64]{0:T(128)} copy(f32[64]{0:T(128)} %bitcast.5) | data formatting | bytes 512
  65.8 1.7 %copy.17 = f32[32,2560]{1,0:T(8,128)} copy(f32[32,2560]{1,0:T(8,128)} %get-tuple-element.14) | data formatting | bytes 655360

commit v2 on v1

--- a/solution.py
+++ b/solution.py
@@ -29,10 +29,10 @@
     n,
     q_ref, k_ref, v_ref, h_ref, gain_ref, list_ref, count_ref, a_hbm, bias_ref,
     ctx_ref, col_ref, out_ref,
-    a_ref, kbuf, vbuf, s_ref, e_ref, sel_send, sel_recv, g_ref, comp_ref,
-    y_send, y_recv, own_ref, z_send, z_recv, c_send, c_recv, ct_send, ct_recv,
-    a_sem, kv_ssem, kv_rsem, sv_ssem, sv_rsem, fw_ssem, fw_rsem,
-    y_ssem, y_rsem, z_ssem, z_rsem, c_ssem, c_rsem, ct_ssem, ct_rsem,
+    a_ref, kvbuf, s_ref, e_ref, sel_send, sel_recv, g_ref, comp_ref,
+    y_send, y_recv, own_ref, x_send, x_recv, z_send, z_recv, c_send, c_recv, ct_send, ct_recv,
+    a_sem, kz_ssem, kz_rsem, ky_ssem, ky_rsem, sv_ssem, sv_rsem, fw_ssem, fw_rsem,
+    y_ssem, y_rsem, x_ssem, x_rsem, z_ssem, z_rsem, c_ssem, c_rsem, ct_ssem, ct_rsem,
 ):
     me = lax.axis_index("seq")
     ten = lax.axis_index("ten")
@@ -50,13 +50,15 @@
     parity = lax.rem(me, 2)
     pair = lax.div(me, 2)
     partner = {"seq": me + 1 - 2 * parity}
+    quads = pairs // 2
+    pair_parity = lax.rem(pair, 2)
+    other_pair = pair + 1 - 2 * pair_parity
 
     a_copy = pltpu.make_async_copy(a_hbm, a_ref, a_sem)
     a_copy.start()
-    kbuf[...] = jnp.zeros_like(kbuf)
-    vbuf[...] = jnp.zeros_like(vbuf)
-    kbuf[me] = k_ref[...]
-    vbuf[me] = v_ref[...]
+    kvbuf[...] = jnp.zeros_like(kvbuf)
+    kvbuf[me, 0] = k_ref[...]
+    kvbuf[me, 1] = v_ref[...]
 
     barrier = pltpu.get_barrier_semaphore()
     for d in range(1, n):
@@ -69,18 +71,42 @@
     )
     pl.semaphore_wait(barrier, n)
 
-    def kv_copies(d, source, target):
-        return (
-            remote(k_ref, kbuf.at[source], kv_ssem.at[0, d], kv_rsem.at[0, d], {"seq": target}),
-            remote(v_ref, vbuf.at[source], kv_ssem.at[1, d], kv_rsem.at[1, d], {"seq": target}),
-        )
-
-    for d in range(1, n):
-
-        @pl.when(me + d < n)
-        def _():
-            for copy in kv_copies(d, me, me + d):
-                copy.start()
+    def chain(age):
+        block = kvbuf.at[2 * (pair - age) + parity]
+        target = {"seq": me + 2}
+        return remote(block, block, kz_ssem.at[age], kz_rsem.at[age + 1], target)
+
+    def chain_in(age):
+        block = kvbuf.at[2 * (pair - age) + parity]
+        return remote(block, block, kz_ssem.at[age - 1], kz_rsem.at[age], partner)
+
+    def across(age):
+        block = kvbuf.at[2 * (pair - age) + parity]
+        return remote(block, block, ky_ssem.at[age], ky_rsem.at[age], partner)
+
+    def across_in(age):
+        block = kvbuf.at[2 * (pair - age) + 1 - parity]
+        return remote(block, block, ky_ssem.at[age], ky_rsem.at[age], partner)
+
+    @pl.when(pair + 1 < pairs)
+    def _():
+        chain(0).start()
+
+    @pl.when(parity == 0)
+    def _():
+        across(0).start()
+
+    def relay(age):
+        @pl.when(pair >= age)
+        def _():
+            chain_in(age).wait_recv()
+            across(age).start()
+
+        if age + 1 < pairs:
+
+            @pl.when((pair >= age) & (pair + 1 < pairs))
+            def _():
+                chain(age).start()
 
     square = jnp.zeros((rows, 1), F32)
     step = math.gcd(width, 1024)
@@ -103,10 +129,13 @@
             sel_send.at[d], sel_recv.at[ten, source], sv_ssem.at[d], sv_rsem.at[d], {"seq": target}
         )
 
-    for d in range(1, n):
+    order = sorted(range(1, n), key=lambda d: abs(2 * d - n))
+    for at, d in enumerate(order):
         owner = lax.rem(me + d, n)
         sel_send[d] = chosen(owner)
         sel_copy(d, me, owner).start()
+        if at % 2 == 1 and at // 2 + 1 < pairs:
+            relay(at // 2 + 1)
     sel_recv[ten, me] = chosen(me)
 
     def forward(d):
@@ -127,18 +156,22 @@
     for side in range(2):
         side_parity = 1 - parity if side == 0 else parity
         for d in range(pairs):
-            base = (2 * lax.rem(pair + d, pairs) + side_parity) * out_rows
+            origin = other_pair if d < quads else pair
+            base = (2 * lax.rem(origin + 2 * (d % quads), pairs) + side_parity) * out_rows
             first = (side * pairs + d) * out_rows
             g_ref[first:first + out_rows, :] = (
                 (row_at + base == place).astype(F32).astype(BF16)
             )
 
-    for d in range(1, n):
-
-        @pl.when(me - d >= 0)
-        def _():
-            for copy in kv_copies(d, me - d, me):
-                copy.wait_recv()
+    @pl.when(parity == 1)
+    def _():
+        across_in(0).wait_recv()
+
+    for age in range(1, pairs):
+
+        @pl.when(pair >= age)
+        def _():
+            across_in(age).wait_recv()
 
     key_pos = lax.broadcasted_iota(jnp.int32, (rows, key_total), 1)
     query_pos = me * rows + lax.broadcasted_iota(jnp.int32, (rows, key_total), 0)
@@ -153,8 +186,8 @@
             ],
             axis=0,
         )
-        key = kbuf[:, :, heads].reshape(key_total, HEAD_SIZE)
-        value = vbuf[:, :, heads].reshape(key_total, HEAD_SIZE)
+        key = kvbuf[:, 0, :, heads].reshape(key_total, HEAD_SIZE)
+        value = kvbuf[:, 1, :, heads].reshape(key_total, HEAD_SIZE)
         s_ref[...] = lax.dot_general(
             query, key, (((1,), (1,)), ((), ())), preferred_element_type=F32
         )
@@ -193,7 +226,7 @@
         def _():
             col_copy(d, me - d, me - d).start()
 
-    for d in range(1, n):
+    for d in order:
         sel_copy(d, lax.rem(me - d + n, n), me).wait_recv()
         forward(d).start()
     for d in range(n):
@@ -211,18 +244,39 @@
     def y_copy(c):
         return remote(y_send.at[c], y_recv.at[c], y_ssem.at[c], y_rsem.at[c], partner)
 
+    def x_copy(c):
+        target = {"seq": 2 * other_pair + parity}
+        return remote(x_send.at[c], x_recv.at[c], x_ssem.at[c], x_rsem.at[c], target)
+
     def z_copy(c, d):
-        target = {"seq": 2 * lax.rem(pair + d, pairs) + parity}
+        target = {"seq": 2 * lax.rem(pair + 2 * d, pairs) + parity}
         return remote(
             z_send.at[c, d], z_recv.at[c, d], z_ssem.at[c, d], z_rsem.at[c, d], target
         )
 
-    def pass_on(c):
+    quad_rows = quads * out_rows
+
+    def to_other_pair(c):
         y_copy(c).wait_recv()
-        for d in range(1, pairs):
-            part = slice(d * out_rows, (d + 1) * out_rows)
-            z_send[c, d] = (own_ref[c, part, :] + y_recv[c, part, :].astype(F32)).astype(BF16)
-            z_copy(c, d).start()
+        x_send[c] = (
+            own_ref[c, :quad_rows, :] + y_recv[c, :quad_rows, :].astype(F32)
+        ).astype(BF16)
+        x_copy(c).start()
+
+    def to_owners(c):
+        x_copy(c).wait_recv()
+        for d in range(quads):
+            part = slice(quad_rows + d * out_rows, quad_rows + (d + 1) * out_rows)
+            total = (
+                own_ref[c, part, :]
+                + y_recv[c, part, :].astype(F32)
+                + x_recv[c, d * out_rows:(d + 1) * out_rows, :].astype(F32)
+            )
+            if d == 0:
+                own_ref[c, part, :] = total
+            else:
+                z_send[c, d] = total.astype(BF16)
+                z_copy(c, d).start()
 
     for c in range(chunks):
         columns = slice(c * chunk, (c + 1) * chunk)
@@ -233,11 +287,12 @@
         own_ref[c] = jnp.dot(
             comp_ref[side_rows:, :], a_ref[:, columns], preferred_element_type=F32
         )
+    for c in range(chunks):
+        to_other_pair(c)
         if c > 0:
-            pass_on(c - 1)
-    pass_on(chunks - 1)
-
-    zero = jnp.int32(0)
+            to_owners(c - 1)
+    to_owners(chunks - 1)
+
     mine = c_send[lax.div(me, per)]
     for d in range(1, n):
         c_recv_valid = me + d < n
@@ -257,11 +312,11 @@
 
     for c in range(chunks):
         columns = slice(c * chunk, (c + 1) * chunk)
-        total = own_ref[c, :out_rows, :] + y_recv[c, :out_rows, :].astype(F32)
-        for d in range(1, pairs):
+        total = own_ref[c, quad_rows:quad_rows + out_rows, :]
+        for d in range(1, quads):
             z_copy(c, d).wait_recv()
             total = total + z_recv[c, d].astype(F32)
-        out_ref[:, columns] = total + bias_ref[:, columns]
+        out_ref[:, columns] = total + bias_ref[columns].reshape(1, chunk)
 
     ct.wait()
     both = jnp.sum(ct_send[...] + ct_recv[...], axis=0, keepdims=True) / QUERY_HEADS
@@ -273,22 +328,44 @@
 
     for d in range(1, n):
 
-        @pl.when(me + d < n)
-        def _():
-            for copy in kv_copies(d, me, me + d):
-                copy.wait_send()
-
         @pl.when(me - d >= 0)
         def _():
             col_copy(d, me - d, me - d).wait_send()
 
         sel_copy(d, me, lax.rem(me + d, n)).wait_send()
+    @pl.when(parity == 0)
+    def _():
+        across(0).wait_send()
+
+    @pl.when(pair + 1 < pairs)
+    def _():
+        chain(0).wait_send()
+
+    for age in range(1, pairs):
+
+        @pl.when(pair >= age)
+        def _():
+            across(age).wait_send()
+
+        if age + 1 < pairs:
+
+            @pl.when((pair >= age) & (pair + 1 < pairs))
+            def _():
+                chain(age).wait_send()
+
     for d in range(n):
         forward(d).wait_send()
     for c in range(chunks):
         y_copy(c).wait_send()
-        for d in range(1, pairs):
+        x_copy(c).wait_send()
+        for d in range(1, quads):
             z_copy(c, d).wait_send()
+
+
+def hand_over(context, scores, projected, context_out, scores_out, projected_out):
+    context_out[...] = context[...]
+    scores_out[...] = scores[...]
+    projected_out[...] = projected[...]
 
 
 def shards(
@@ -306,6 +383,7 @@
     chunk = math.gcd(columns, 512)
     chunks = columns // chunk
     pairs = n // 2
+    quads = n // 4
     lanes = max(128, rows)
     key_total = n * rows
     vmem = pl.BlockSpec(memory_space=pltpu.VMEM)
@@ -326,8 +404,7 @@
         out_specs=(vmem, vmem, vmem),
         scratch_shapes=[
             pltpu.VMEM((depth, columns), BF16),
-            pltpu.VMEM((n, rows, kv_width), BF16),
-            pltpu.VMEM((n, rows, kv_width), BF16),
+            pltpu.VMEM((n, 2, rows, kv_width), BF16),
             pltpu.VMEM((group * rows, key_total), F32),
             pltpu.VMEM((group * rows, key_total), BF16),
             pltpu.VMEM((n, rows, half), BF16),
@@ -337,18 +414,22 @@
             pltpu.VMEM((chunks, kept_total // 2, chunk), BF16),
             pltpu.VMEM((chunks, kept_total // 2, chunk), BF16),
             pltpu.VMEM((chunks, kept_total // 2, chunk), F32),
-            pltpu.VMEM((chunks, pairs, out_rows, chunk), BF16),
-            pltpu.VMEM((chunks, pairs, out_rows, chunk), BF16),
+            pltpu.VMEM((chunks, kept_total // 4, chunk), BF16),
+            pltpu.VMEM((chunks, kept_total // 4, chunk), BF16),
+            pltpu.VMEM((chunks, quads, out_rows, chunk), BF16),
+            pltpu.VMEM((chunks, quads, out_rows, chunk), BF16),
             pltpu.VMEM((key_total // lanes, 8, lanes), F32),
             pltpu.VMEM((n, 8, lanes), F32),
             pltpu.VMEM((8, lanes), F32),
             pltpu.VMEM((8, lanes), F32),
             dma,
-            dma((2, n)), dma((2, n)),
+            dma((pairs,)), dma((pairs,)),
+            dma((pairs,)), dma((pairs,)),
             dma((n,)), dma((n,)),
             dma((n,)), dma((n,)),
             dma((chunks,)), dma((chunks,)),
-            dma((chunks, pairs)), dma((chunks, pairs)),
+            dma((chunks,)), dma((chunks,)),
+            dma((chunks, quads)), dma((chunks, quads)),
             dma((n,)), dma((n,)),
             dma, dma,
         ],
@@ -356,8 +437,18 @@
     )(
         queries, keys, values, hidden, norm_gain.reshape(1, width),
         retained_lists.reshape(1, rows), counts, affine_matrix,
-        affine_offset_vector.reshape(1, columns),
+        affine_offset_vector,
     )
+    context, col_scores, projected = pl.pallas_call(
+        hand_over,
+        out_shape=(
+            jax.ShapeDtypeStruct(context.shape, F32),
+            jax.ShapeDtypeStruct(col_scores.shape, F32),
+            jax.ShapeDtypeStruct(projected.shape, F32),
+        ),
+        in_specs=[vmem, vmem, vmem],
+        out_specs=(vmem, vmem, vmem),
+    )(context, col_scores, projected)
     return (context, col_scores.reshape(rows), projected)
 
 

time: 67.8 us -> 56.8 us (0.84)
  local copies, waits for them, and re-layouts: 6.07 us -> 0 us
  Pallas kernels: 60.8 us -> 56 us
    pallas_call x1, Pallas kernels: 60.8 us -> 53.9 us  [shards(): pl.pallas_call(functools.partial(kernel, n), out_shape=(jax.ShapeDtypeStr...]
    unnamed x3 -> x0, local copies, waits for them, and re-layouts: 4.76 us -> none
    pallas_call x0 -> x1, Pallas kernels: none -> 2.07 us  [shards(): pl.pallas_call(hand_over, out_shape=(jax.ShapeDtypeStruct(context.shape,...]
    reshape x1 -> x0, local copies, waits for them, and re-layouts: 1.31 us -> none  [shards(): affine_offset_vector.reshape(1, columns)]
where the time goes in v2:
time: 56.8 us; the launch traced here: 56.6 us
  Pallas kernels  56 us (99%)
  between operations  0.64 us (1%)
    pallas_call x1, Pallas kernels, shards(): pl.pallas_call(functools.partial(kernel, n), out_shape=(jax.ShapeDtypeStr...  53.9 us
    pallas_call x1, Pallas kernels, shards(): pl.pallas_call(hand_over, out_shape=(jax.ShapeDtypeStruct(context.shape,...  2.07 us

profile of v2, /device:TPU:0, one launch (start us, length us, event | category | flops | bytes accessed | tf_op | source)
XLA Modules:
  0.0 56.6 jit_solution(13393149993625245352)
XLA Ops:
  0.6 53.9 %shard_map.112 = (f32[64,2048]{1,0:T(8,128)}, f32[1,64]{1,0:T(1,128)}, f32[32,2560]{1,0:T(8,128)}) custom-call(bf16[64,2048]{1,0:T(8,128)(2,1)} %q_ref.1, bf16[64,256]{1,0:T(8,128)(2,1)} %k_ref.1, bf16[64,256]{1,0:T(8,128)(2,1)} %v_ref.1, bf16[64,8192]{1,0:T(8,128)(2,1)} %h_ref.1, f32[1,8192]{1,0:T(1,128)} %bitcast.3, s32[1,64]{1,0:T(1,128)} %bitcast.4, ...), custom_call_target="tpu_custom_call" | custom-call | tf_op jit(solution)/shard_map/pallas_call | solution.py:391
  54.5 2.1 %shard_map.113 = (f32[64,2048]{1,0:T(8,128)}, f32[1,64]{1,0:T(1,128)}, f32[32,2560]{1,0:T(8,128)}) custom-call(f32[64,2048]{1,0:T(8,128)} %get-tuple-element.9.context, f32[1,64]{1,0:T(1,128)} %get-tuple-element.10.scores, f32[32,2560]{1,0:T(8,128)} %get-tuple-element.11.projected), custom_call_target="tpu_custom_call" | custom-call | tf_op jit(solution)/shard_map/pallas_call | solution.py:442

commit v3 on v2

--- a/solution.py
+++ b/solution.py
@@ -130,12 +130,10 @@
         )
 
     order = sorted(range(1, n), key=lambda d: abs(2 * d - n))
-    for at, d in enumerate(order):
+    for d in order:
         owner = lax.rem(me + d, n)
         sel_send[d] = chosen(owner)
         sel_copy(d, me, owner).start()
-        if at % 2 == 1 and at // 2 + 1 < pairs:
-            relay(at // 2 + 1)
     sel_recv[ten, me] = chosen(me)
 
     def forward(d):
@@ -162,6 +160,68 @@
             g_ref[first:first + out_rows, :] = (
                 (row_at + base == place).astype(F32).astype(BF16)
             )
+
+    relay(1)
+    for at, d in enumerate(order):
+        sel_copy(d, lax.rem(me - d + n, n), me).wait_recv()
+        forward(d).start()
+        if at % 2 == 0 and 0 < at < n - 2:
+            relay(at // 2 + 1)
+    for d in range(n):
+        source = lax.rem(me - d + n, n)
+        block = sel_recv.at[1 - ten, source]
+        remote(block, block, fw_ssem.at[d], fw_rsem.at[d], sibling).wait_recv()
+    for side in range(2):
+        comp_ref[:, side * half:(side + 1) * half] = jnp.dot(
+            g_ref[...], sel_recv[side].reshape(key_total, half), preferred_element_type=F32
+        ).astype(BF16)
+    a_copy.wait()
+
+    side_rows = pairs * out_rows
+
+    def y_copy(c):
+        return remote(y_send.at[c], y_recv.at[c], y_ssem.at[c], y_rsem.at[c], partner)
+
+    def x_copy(c):
+        target = {"seq": 2 * other_pair + parity}
+        return remote(x_send.at[c], x_recv.at[c], x_ssem.at[c], x_rsem.at[c], target)
+
+    def z_copy(c, d):
+        target = {"seq": 2 * lax.rem(pair + 2 * d, pairs) + parity}
+        return remote(
+            z_send.at[c, d], z_recv.at[c, d], z_ssem.at[c, d], z_rsem.at[c, d], target
+        )
+
+    quad_rows = quads * out_rows
+
+    def to_other_pair(c):
+        y_copy(c).wait_recv()
+        x_send[c] = (
+            own_ref[c, :quad_rows, :] + y_recv[c, :quad_rows, :].astype(F32)
+        ).astype(BF16)
+        x_copy(c).start()
+
+    def to_owners(c):
+        x_copy(c).wait_recv()
+        for d in range(quads):
+            part = slice(quad_rows + d * out_rows, quad_rows + (d + 1) * out_rows)
+            total = (
+                own_ref[c, part, :]
+                + y_recv[c, part, :].astype(F32)
+                + x_recv[c, d * out_rows:(d + 1) * out_rows, :].astype(F32)
+            )
+            if d == 0:
+                own_ref[c, part, :] = total
+            else:
+                z_send[c, d] = total.astype(BF16)
+                z_copy(c, d).start()
+
+    for c in range(chunks):
+        columns = slice(c * chunk, (c + 1) * chunk)
+        part = jnp.dot(comp_ref[...], a_ref[:, columns], preferred_element_type=F32)
+        y_send[c] = part[:side_rows].astype(BF16)
+        y_copy(c).start()
+        own_ref[c] = part[side_rows:]
 
     @pl.when(parity == 1)
     def _():
@@ -226,67 +286,6 @@
         def _():
             col_copy(d, me - d, me - d).start()
 
-    for d in order:
-        sel_copy(d, lax.rem(me - d + n, n), me).wait_recv()
-        forward(d).start()
-    for d in range(n):
-        source = lax.rem(me - d + n, n)
-        block = sel_recv.at[1 - ten, source]
-        remote(block, block, fw_ssem.at[d], fw_rsem.at[d], sibling).wait_recv()
-    for side in range(2):
-        comp_ref[:, side * half:(side + 1) * half] = jnp.dot(
-            g_ref[...], sel_recv[side].reshape(key_total, half), preferred_element_type=F32
-        ).astype(BF16)
-    a_copy.wait()
-
-    side_rows = pairs * out_rows
-
-    def y_copy(c):
-        return remote(y_send.at[c], y_recv.at[c], y_ssem.at[c], y_rsem.at[c], partner)
-
-    def x_copy(c):
-        target = {"seq": 2 * other_pair + parity}
-        return remote(x_send.at[c], x_recv.at[c], x_ssem.at[c], x_rsem.at[c], target)
-
-    def z_copy(c, d):
-        target = {"seq": 2 * lax.rem(pair + 2 * d, pairs) + parity}
-        return remote(
-            z_send.at[c, d], z_recv.at[c, d], z_ssem.at[c, d], z_rsem.at[c, d], target
-        )
-
-    quad_rows = quads * out_rows
-
-    def to_other_pair(c):
-        y_copy(c).wait_recv()
-        x_send[c] = (
-            own_ref[c, :quad_rows, :] + y_recv[c, :quad_rows, :].astype(F32)
-        ).astype(BF16)
-        x_copy(c).start()
-
-    def to_owners(c):
-        x_copy(c).wait_recv()
-        for d in range(quads):
-            part = slice(quad_rows + d * out_rows, quad_rows + (d + 1) * out_rows)
-            total = (
-                own_ref[c, part, :]
-                + y_recv[c, part, :].astype(F32)
-                + x_recv[c, d * out_rows:(d + 1) * out_rows, :].astype(F32)
-            )
-            if d == 0:
-                own_ref[c, part, :] = total
-            else:
-                z_send[c, d] = total.astype(BF16)
-                z_copy(c, d).start()
-
-    for c in range(chunks):
-        columns = slice(c * chunk, (c + 1) * chunk)
-        y_send[c] = jnp.dot(
-            comp_ref[:side_rows, :], a_ref[:, columns], preferred_element_type=F32
-        ).astype(BF16)
-        y_copy(c).start()
-        own_ref[c] = jnp.dot(
-            comp_ref[side_rows:, :], a_ref[:, columns], preferred_element_type=F32
-        )
     for c in range(chunks):
         to_other_pair(c)
         if c > 0:

time: 56.8 us -> 54.2 us (0.954)
  Pallas kernels: 56 us -> 53.4 us
    pallas_call x1, Pallas kernels: 53.9 us -> 51.4 us  [shards(): pl.pallas_call(functools.partial(kernel, n), out_shape=(jax.ShapeDtypeStr...]
where the time goes in v3:
time: 54.2 us; the launch traced here: 54.1 us
  Pallas kernels  53.4 us (99%)
  between operations  0.64 us (1%)
    pallas_call x1, Pallas kernels, shards(): pl.pallas_call(functools.partial(kernel, n), out_shape=(jax.ShapeDtypeStr...  51.4 us
    pallas_call x1, Pallas kernels, shards(): pl.pallas_call(hand_over, out_shape=(jax.ShapeDtypeStruct(context.shape,...  2.07 us

profile of v3, /device:TPU:0, one launch (start us, length us, event | category | flops | bytes accessed | tf_op | source)
XLA Modules:
  0.0 54.1 jit_solution(9432740758798396436)
XLA Ops:
  0.6 51.4 %shard_map.112 = (f32[64,2048]{1,0:T(8,128)}, f32[1,64]{1,0:T(1,128)}, f32[32,2560]{1,0:T(8,128)}) custom-call(bf16[64,2048]{1,0:T(8,128)(2,1)} %q_ref.1, bf16[64,256]{1,0:T(8,128)(2,1)} %k_ref.1, bf16[64,256]{1,0:T(8,128)(2,1)} %v_ref.1, bf16[64,8192]{1,0:T(8,128)(2,1)} %h_ref.1, f32[1,8192]{1,0:T(1,128)} %bitcast.3, s32[1,64]{1,0:T(1,128)} %bitcast.4, ...), custom_call_target="tpu_custom_call" | custom-call | tf_op jit(solution)/shard_map/pallas_call | solution.py:390
  52.0 2.1 %shard_map.113 = (f32[64,2048]{1,0:T(8,128)}, f32[1,64]{1,0:T(1,128)}, f32[32,2560]{1,0:T(8,128)}) custom-call(f32[64,2048]{1,0:T(8,128)} %get-tuple-element.9.context, f32[1,64]{1,0:T(1,128)} %get-tuple-element.10.scores, f32[32,2560]{1,0:T(8,128)} %get-tuple-element.11.projected), custom_call_target="tpu_custom_call" | custom-call | tf_op jit(solution)/shard_map/pallas_call | solution.py:441

commit v4 on v3

--- a/solution.py
+++ b/solution.py
@@ -177,13 +177,15 @@
         ).astype(BF16)
     a_copy.wait()
 
-    side_rows = pairs * out_rows
+
+    other = {"seq": 2 * other_pair + parity}
 
     def y_copy(c):
-        return remote(y_send.at[c], y_recv.at[c], y_ssem.at[c], y_rsem.at[c], partner)
+        target = other if c == 0 else partner
+        return remote(y_send.at[c], y_recv.at[c], y_ssem.at[c], y_rsem.at[c], target)
 
     def x_copy(c):
-        target = {"seq": 2 * other_pair + parity}
+        target = partner if c == 0 else other
         return remote(x_send.at[c], x_recv.at[c], x_ssem.at[c], x_rsem.at[c], target)
 
     def z_copy(c, d):
@@ -219,9 +221,14 @@
     for c in range(chunks):
         columns = slice(c * chunk, (c + 1) * chunk)
         part = jnp.dot(comp_ref[...], a_ref[:, columns], preferred_element_type=F32)
-        y_send[c] = part[:side_rows].astype(BF16)
+        quarters = [part[i * quad_rows:(i + 1) * quad_rows] for i in range(4)]
+        away, stay = ((0, 2), (1, 3)) if c == 0 else ((0, 1), (2, 3))
+        for i in range(2):
+            lines = slice(i * quad_rows, (i + 1) * quad_rows)
+            y_send[c, lines, :] = quarters[away[i]].astype(BF16)
         y_copy(c).start()
-        own_ref[c] = part[side_rows:]
+        for i in range(2):
+            own_ref[c, i * quad_rows:(i + 1) * quad_rows, :] = quarters[stay[i]]
 
     @pl.when(parity == 1)
     def _():
@@ -286,11 +293,14 @@
         def _():
             col_copy(d, me - d, me - d).start()
 
-    for c in range(chunks):
+    to_other_pair(0)
+    for c in range(1, chunks):
         to_other_pair(c)
-        if c > 0:
+        if c > 1:
             to_owners(c - 1)
-    to_owners(chunks - 1)
+    if chunks > 1:
+        to_owners(chunks - 1)
+    to_owners(0)
 
     mine = c_send[lax.div(me, per)]
     for d in range(1, n):

time: 54.2 us -> 53.1 us (0.980)
  Pallas kernels: 53.4 us -> 52.2 us
    pallas_call x1, Pallas kernels: 51.4 us -> 50.2 us  [shards(): pl.pallas_call(functools.partial(kernel, n), out_shape=(jax.ShapeDtypeStr...]
where the time goes in v4:
time: 53.1 us; the launch traced here: 52.9 us
  Pallas kernels  52.2 us (98%)
  between operations  0.64 us (1%)
    pallas_call x1, Pallas kernels, shards(): pl.pallas_call(functools.partial(kernel, n), out_shape=(jax.ShapeDtypeStr...  50.2 us
    pallas_call x1, Pallas kernels, shards(): pl.pallas_call(hand_over, out_shape=(jax.ShapeDtypeStruct(context.shape,...  2.07 us

profile of v4, /device:TPU:0, one launch (start us, length us, event | category | flops | bytes accessed | tf_op | source)
XLA Modules:
  0.0 52.9 jit_solution(2814363247254738424)
XLA Ops:
  0.6 50.2 %shard_map.112 = (f32[64,2048]{1,0:T(8,128)}, f32[1,64]{1,0:T(1,128)}, f32[32,2560]{1,0:T(8,128)}) custom-call(bf16[64,2048]{1,0:T(8,128)(2,1)} %q_ref.1, bf16[64,256]{1,0:T(8,128)(2,1)} %k_ref.1, bf16[64,256]{1,0:T(8,128)(2,1)} %v_ref.1, bf16[64,8192]{1,0:T(8,128)(2,1)} %h_ref.1, f32[1,8192]{1,0:T(1,128)} %bitcast.3, s32[1,64]{1,0:T(1,128)} %bitcast.4, ...), custom_call_target="tpu_custom_call" | custom-call | tf_op jit(solution)/shard_map/pallas_call | solution.py:400
  50.8 2.1 %shard_map.113 = (f32[64,2048]{1,0:T(8,128)}, f32[1,64]{1,0:T(1,128)}, f32[32,2560]{1,0:T(8,128)}) custom-call(f32[64,2048]{1,0:T(8,128)} %get-tuple-element.9.context, f32[1,64]{1,0:T(1,128)} %get-tuple-element.10.scores, f32[32,2560]{1,0:T(8,128)} %get-tuple-element.11.projected), custom_call_target="tpu_custom_call" | custom-call | tf_op jit(solution)/shard_map/pallas_call | solution.py:451
